TPU v7x, 32 devices: a whole 2x2x4 slice. The times are simulated.
32 devices in a mesh: parts: 2 (over x), dp: 4 (over y, core), shard: 4 (over z).
Axes of the slice: x: 2, y: 2, z: 4, core: 2. Of those that a mesh axis runs over, the one named last changes fastest.
Arguments:
- projected: bfloat16 [7680, 7680], P(('parts', 'dp', 'shard')), parts along dimension 0, may hold values from -4 to 4
- residual: bfloat16 [7680, 2560], P(('parts', 'dp', 'shard')), parts along dimension 0, may hold values from -6 to 6
- out_weight: bfloat16 [2560, 2560], P(None, 'shard'), may hold values from -0.125 to 0.125
- probe_weight: bfloat16 [2, 2560, 8], replicated, may hold values from -0.125 to 0.125
- labels: int32 [7680], P(('parts', 'dp', 'shard')), parts along dimension 0, may hold values from 0 to 7
- lengths: int32 [32, 9], P(('parts', 'dp', 'shard')), parts along dimension 0, may hold values from 12 to 48, as said below
- destination: int32 [32, 9], P(('parts', 'dp', 'shard')), parts along dimension 0, may hold values from 0 to 3, as said below
Outputs:
- hidden_rows: bfloat16 [18432, 2560], P(('parts', 'dp', 'shard')), parts along dimension 0
- probe_grad: float32 [4, 2560, 8], P('parts'), parts along dimension 0
There are 2 independent parts, one for each index of `parts`. A program takes and returns all parts, laid end to end along the dimension named above; an argument that names none is the same for every part. Nothing has to cross between parts.
Inputs may be any that keep to these rules, and one draw needn't show every extreme that they name: Each row of lengths sums to 240 and holds exactly one protein of length 48. `destination`: A loader assigns at most 3 proteins to any one dp index; in every shard column one dp index is assigned exactly 3 proteins by every loader of that column.
All inputs are finite; a program needn't handle non-finite values.
Results may differ from a plain program's by a relative error of at most 0.0031.
Values may be sent and summed in bfloat16 or wider, within the bound.
No kernel may reach another device: no remote copies, remote signals or barrier semaphores. Data moves between devices by JAX's collectives and lax.ppermute only.
A program may use at most 128 MiB of HBM per device.

v0:
```python
import jax
import jax.numpy as jnp
from jax import lax
from jax.sharding import PartitionSpec as P

HS = 128
CLASSES = 8
LMAX = 48
TOK_DEV = 240


def attend(blocks, block_lengths):
    block_count = blocks.shape[0]
    span_rows = blocks.shape[1]
    head_width = blocks.shape[2] // 3
    head_count = head_width // HS
    queries = blocks[:, :, :head_width].reshape(block_count, span_rows, head_count, HS)
    key_rows = blocks[:, :, head_width : 2 * head_width].reshape(
        block_count, span_rows, head_count, HS
    )
    value_rows = blocks[:, :, 2 * head_width :].reshape(block_count, span_rows, head_count, HS)
    scores = jnp.einsum(
        "plhs,pmhs->phlm", queries, key_rows, preferred_element_type=jnp.float32
    ) * HS ** (-0.5)
    keep_mask = (jnp.arange(span_rows, dtype=jnp.int32)[None, :] < block_lengths[:, None]).astype(
        jnp.float32
    )
    weights = jnp.exp(scores) * keep_mask[:, None, None, :]
    denominator = (
        jnp.sum(weights, axis=-1, keepdims=True)
        + (block_lengths == 0).astype(jnp.float32)[:, None, None, None]
    )
    weight_low = (weights / denominator).astype(jnp.bfloat16)
    attended = jnp.einsum(
        "phlm,pmhs->plhs", weight_low, value_rows, preferred_element_type=jnp.float32
    )
    return attended.reshape(block_count * span_rows, head_width).astype(jnp.bfloat16)


def project(attended, out_weight):
    return jnp.dot(
        attended,
        lax.all_gather(out_weight, "shard", axis=1, tiled=True),
        preferred_element_type=jnp.float32,
    )


def probe_terms(represent_x, represent_h, label_rows, keep_mask, probe_weight):
    one_hot = (label_rows[:, None] == jnp.arange(CLASSES, dtype=jnp.int32)[None, :]).astype(
        jnp.float32
    )
    collected = []
    for which, represent in enumerate((represent_x, represent_h)):
        logits = jnp.dot(represent, probe_weight[which], preferred_element_type=jnp.float32)
        exponent = jnp.exp(logits)
        likelihood = exponent / jnp.sum(exponent, axis=1, keepdims=True)
        mismatch = ((likelihood - one_hot) * keep_mask[:, None] / TOK_DEV).astype(jnp.bfloat16)
        collected.append(
            lax.dot_general(
                represent, mismatch, (((0,), (0,)), ((), ())), preferred_element_type=jnp.float32
            )
        )
    return jnp.stack(collected)


def per_device(projected, residual, out_weight, probe_weight, labels, lengths, destination):
    group_size = lax.axis_size("dp")
    prot_count = lengths.shape[1]
    slot_count = -(-prot_count // group_size)
    tok_count = projected.shape[0]
    lens_own = lengths[0]
    dest_own = destination[0]
    starts = jnp.cumsum(lens_own) - lens_own
    offsets = jnp.arange(LMAX, dtype=jnp.int32)
    positions = jnp.arange(prot_count, dtype=jnp.int32)
    same_dest = dest_own[:, None] == dest_own[None, :]
    earlier = positions[:, None] > positions[None, :]
    slot_rank = jnp.sum((same_dest & earlier).astype(jnp.int32), axis=1)
    slot_match = (
        dest_own[None, None, :] == jnp.arange(group_size, dtype=jnp.int32)[:, None, None]
    ) & (slot_rank[None, None, :] == jnp.arange(slot_count, dtype=jnp.int32)[None, :, None])
    match_int = slot_match.astype(jnp.int32)
    slot_start = jnp.sum(match_int * starts, axis=2)
    slot_len = jnp.sum(match_int * lens_own, axis=2)
    block_count = group_size * slot_count
    row_index = jnp.minimum(slot_start[:, :, None] + offsets, tok_count - 1).reshape(
        group_size, slot_count * LMAX
    )
    live_rows = (offsets[None, None, :] < slot_len[:, :, None]).reshape(
        group_size, slot_count * LMAX
    )
    rows_send = jnp.where(live_rows[:, :, None], jnp.take(projected, row_index, axis=0), 0)
    resid_send = jnp.where(live_rows[:, :, None], jnp.take(residual, row_index, axis=0), 0)
    label_send = jnp.where(live_rows, jnp.take(labels, row_index), 0)
    got_labels, got_lengths = (
        lax.all_to_all(label_send, "dp", split_axis=0, concat_axis=0, tiled=True),
        lax.all_to_all(slot_len, "dp", split_axis=0, concat_axis=0, tiled=True),
    )
    got_rows, got_resid = (
        lax.all_to_all(rows_send, "dp", split_axis=0, concat_axis=0, tiled=True),
        lax.all_to_all(resid_send, "dp", split_axis=0, concat_axis=0, tiled=True),
    )
    lengths_recv = got_lengths.reshape(block_count)
    attended = attend(got_rows.reshape(block_count, LMAX, -1), lengths_recv)
    keep_mask = (offsets[None, :] < lengths_recv[:, None]).astype(jnp.float32).reshape(-1)
    represent = got_resid.reshape(block_count * LMAX, -1)
    mixed_rows = project(attended, out_weight) + represent.astype(jnp.float32)
    hidden = (mixed_rows * keep_mask[:, None]).astype(jnp.bfloat16)
    grad_terms = probe_terms(represent, hidden, got_labels.reshape(-1), keep_mask, probe_weight)
    grad_sum = lax.psum(grad_terms, ("dp", "shard"))
    return (hidden, grad_sum)


def solution(mesh):
    return jax.shard_map(
        per_device,
        mesh=mesh,
        in_specs=(
            P(("parts", "dp", "shard"), None),
            P(("parts", "dp", "shard"), None),
            P(None, "shard"),
            P(),
            P(("parts", "dp", "shard")),
            P(("parts", "dp", "shard"), None),
            P(("parts", "dp", "shard"), None),
        ),
        out_specs=(P(("parts", "dp", "shard"), None), P("parts", None, None)),
        check_vma=False,
    )
```

profile of v0, /device:TPU:8, one launch (start us, length us, event | category | flops | bytes accessed | tf_op | source)
XLA Modules:
  0.0 349.7 jit_solution(5877579920904036037)
XLA Ops:
  7.2 0.7 all-gather.2.cloned.1.call-update
  8.3 0.2 fusion.37
  8.5 0.7 copy.27
  9.2 3.2 all-to-all-start.1
  13.4 4.2 %gather_fusion.1 = bf16[576,2560]{1,0:T(8,128)(2,1)} fusion(bf16[240,2560]{1,0:T(8,128)(2,1)S(1)} %copy-done, s32[1024]{0:T(1024)S(1)} %pad_clamp_fusion), kind=kCustom, calls=%fused_computation.1 | custom fusion | bytes 5900544 | tf_op jit(solution)/shard_map/jit(_take)/gather | solution.py:93
  17.6 3.9 %gather_fusion.2 = s32[576]{0:T(1024)S(1)} fusion(s32[240]{0:T(256)S(1)} %copy-done.2, s32[1024]{0:T(1024)S(1)} %pad_clamp_fusion), kind=kCustom, calls=%fused_computation.2 | custom fusion | bytes 6912 | tf_op jit(solution)/shard_map/jit(_take)/gather | solution.py:94
  21.6 0.6 copy.31
  22.3 3.3 all-to-all-start.3
  25.5 4.2 %select_select_fusion.1 = bf16[4,144,2560]{2,1,0:T(8,128)(2,1)} fusion(bf16[4,144,2560]{2,1,0:T(8,128)(2,1)} %bitcast.61, pred[4,144]{1,0:T(4,128)(4,1)S(1)} %get-tuple-element.8, pred[4,144]{1,0:T(4,128)(4,1)S(1)} %get-tuple-element.7), kind=kLoop, calls=%fused_computation.23 | loop fusion | flops 2949120 | bytes 5899392 | tf_op jit(solution)/shard_map/jit(_where)/select_n | solution.py:93
  29.7 22.4 %gather_fusion = bf16[576,7680]{1,0:T(8,128)(2,1)} fusion(bf16[240,7680]{1,0:T(8,128)(2,1)} %param.7, s32[1024]{0:T(1024)S(1)} %pad_clamp_fusion), kind=kCustom, calls=%fused_computation | custom fusion | bytes 17697024 | tf_op jit(solution)/shard_map/jit(_take)/gather | solution.py:92
  52.1 4.6 %all-to-all-start.2 = ((bf16[4,144,2560]{2,1,0:T(8,128)(2,1)}), bf16[4,144,2560]{2,1,0:T(8,128)(2,1)}, u32[]{:S(2)}, u32[]{:S(2)}) async-start(bf16[4,144,2560]{2,1,0:T(8,128)(2,1)} %select_select_fusion.1), calls=%async_computation.2 | async-start | bytes 5898240 | tf_op jit(solution)/shard_map/all_to_all | solution.py:101
  56.8 8.1 %select_select_fusion = bf16[4,144,7680]{2,1,0:T(8,128)(2,1)} fusion(bf16[4,144,7680]{2,1,0:T(8,128)(2,1)} %bitcast.60, pred[4,144]{1,0:T(4,128)(4,1)S(1)} %get-tuple-element.8, pred[4,144]{1,0:T(4,128)(4,1)S(1)} %get-tuple-element.7), kind=kLoop, calls=%fused_computation.3 | loop fusion | flops 8847360 | bytes 17695872 | tf_op jit(solution)/shard_map/jit(_where)/select_n | solution.py:92
  64.9 26.7 %all-to-all-done.2 = bf16[4,144,2560]{2,1,0:T(8,128)(2,1)} async-done(((bf16[4,144,2560]{2,1,0:T(8,128)(2,1)}), bf16[4,144,2560]{2,1,0:T(8,128)(2,1)}, u32[]{:S(2)}, u32[]{:S(2)}) %all-to-all-start.2) | async-done | bytes 2949152 | tf_op jit(solution)/shard_map/all_to_all | solution.py:101
  91.6 5.7 %all-to-all-start = ((bf16[4,144,7680]{2,1,0:T(8,128)(2,1)}), bf16[4,144,7680]{2,1,0:T(8,128)(2,1)}, u32[]{:S(2)}, u32[]{:S(2)}) async-start(bf16[4,144,7680]{2,1,0:T(8,128)(2,1)} %select_select_fusion), calls=%async_computation | async-start | bytes 17694720 | tf_op jit(solution)/shard_map/all_to_all | solution.py:100
  97.3 0.2 all-reduce.2.cloned.1.call-start
  97.6 0.5 broadcast.237
  98.1 0.7 reduce.4
  99.1 2.7 fusion.43
  101.8 2.3 convolution_bitcast_fusion.1
  104.1 91.3 %all-to-all-done = bf16[4,144,7680]{2,1,0:T(8,128)(2,1)} async-done(((bf16[4,144,7680]{2,1,0:T(8,128)(2,1)}), bf16[4,144,7680]{2,1,0:T(8,128)(2,1)}, u32[]{:S(2)}, u32[]{:S(2)}) %all-to-all-start) | async-done | bytes 8847392 | tf_op jit(solution)/shard_map/all_to_all | solution.py:100
  195.4 4.0 %slice_bitcast_fusion.2 = (bf16[12,6,20,8,128]{4,3,2,1,0:T(8,128)(2,1)S(1)}, bf16[12,6,20,8,128]{4,3,2,1,0:T(8,128)(2,1)S(1)}, bf16[12,6,20,8,128]{4,3,2,1,0:T(8,128)(2,1)S(1)}) fusion(bf16[12,48,7680]{2,1,0:T(8,128)(2,1)} %bitcast.5), kind=kLoop, calls=%fused_computation.22 | loop fusion | bytes 17694720
  199.4 1.7 fusion
  201.2 2.0 convert_bitcast_fusion
  203.2 2.6 copy.30
  205.8 28.8 %all-gather.2.cloned.1.call-done = bf16[2560,2560]{1,0:T(8,128)(2,1)} async-done(((bf16[2560,640]{1,0:T(8,128)(2,1)}), bf16[2560,2560]{1,0:T(8,128)(2,1)}) %all-gather.2.cloned.1.call-update) | async-done | bytes 13107216 | tf_op jit(solution)/shard_map/all_gather | solution.py:43
  234.6 12.4 %multiply_convert_fusion = bf16[576,2560]{1,0:T(8,128)(2,1)S(1)} fusion(bf16[576,2560]{1,0:T(8,128)(2,1)} %bitcast.9, bf16[2560,2560]{1,0:T(8,128)(2,1)} %all-gather.2.cloned.1.call-done, bf16[72,8,20,128]{3,2,1,0:T(8,128)(2,1)} %bitcast.62, f32[576]{0:T(1024)S(1)} %reshape.360), kind=kOutput, calls=%fused_computation.4 | convolution fusion | flops 7555645440 | bytes 21956864 | tf_op jit(solution)/shard_map/dot_general | solution.py:41
  246.9 0.9 fusion.42
  247.8 0.5 convolution_bitcast_fusion
  248.3 0.2 copy-done.3
  248.5 0.7 pad_maximum_fusion
  249.2 92.0 %all-reduce.2.cloned.1.call-done = f32[2,2560,8]{1,2,0:T(8,128)} async-done(((f32[2,2560,8]{1,2,0:T(8,128)}), f32[2,2560,8]{1,2,0:T(8,128)}) %all-reduce.2.cloned.1.call-update) | async-done | bytes 163856 | tf_op jit(solution)/shard_map/psum | solution.py:110
  341.3 1.6 copy.62
  (46 shorter events, 1.9 us)
Async XLA Ops:
  7.2 6.2 %copy-start = (bf16[240,2560]{1,0:T(8,128)(2,1)S(1)}, bf16[240,2560]{1,0:T(8,128)(2,1)}, u32[]{:S(2)}) copy-start(bf16[240,2560]{1,0:T(8,128)(2,1)} %param.8) | copy-start | bytes 3686404
  7.2 0.8 copy-start.5
  7.2 0.9 copy-start.6
  7.2 227.4 %all-gather.2.cloned.1.call-start = ((), (), s32[]{:S(2)}) async-start(), calls=%async_computation.4 | async-start | bytes 16384000 | tf_op jit(solution)/shard_map/all_gather | solution.py:43
  9.2 13.1 %all-to-all-start.1 = ((s32[4,1,3]{2,1,0:T(1,128)}), s32[4,1,3]{2,1,0:T(1,128)S(1)}, u32[]{:S(2)}, u32[]{:S(2)}) async-start(s32[4,1,3]{2,1,0:T(1,128)} %copy.27), calls=%async_computation.1 | async-start | bytes 4096 | tf_op jit(solution)/shard_map/all_to_all | solution.py:97
  13.4 4.2 %copy-start.2 = (s32[240]{0:T(256)S(1)}, s32[240]{0:T(256)}, u32[]{:S(2)}) copy-start(s32[240]{0:T(256)} %param.11) | copy-start | bytes 2884
  22.3 29.9 %all-to-all-start.3 = ((s32[4,1,144]{2,1,0:T(1,128)}), s32[4,1,144]{2,1,0:T(1,128)S(1)}, u32[]{:S(2)}, u32[]{:S(2)}) async-start(s32[4,1,144]{2,1,0:T(1,128)} %copy.31), calls=%async_computation.3 | async-start | bytes 8192 | tf_op jit(solution)/shard_map/all_to_all | solution.py:96
  52.1 39.5 %all-to-all-start.2 = ((bf16[4,144,2560]{2,1,0:T(8,128)(2,1)}), bf16[4,144,2560]{2,1,0:T(8,128)(2,1)}, u32[]{:S(2)}, u32[]{:S(2)}) async-start(bf16[4,144,2560]{2,1,0:T(8,128)(2,1)} %select_select_fusion.1), calls=%async_computation.2 | async-start | bytes 5898240 | tf_op jit(solution)/shard_map/all_to_all | solution.py:101
  64.9 34.2 %copy-start.4 = (bf16[2,2560,8]{1,2,0:T(8,128)(2,1)S(1)}, bf16[2,2560,8]{1,2,0:T(8,128)(2,1)}, u32[]{:S(2)}) copy-start(bf16[2,2560,8]{1,2,0:T(8,128)(2,1)} %param.10) | copy-start | bytes 245764
  91.6 103.8 %all-to-all-start = ((bf16[4,144,7680]{2,1,0:T(8,128)(2,1)}), bf16[4,144,7680]{2,1,0:T(8,128)(2,1)}, u32[]{:S(2)}, u32[]{:S(2)}) async-start(bf16[4,144,7680]{2,1,0:T(8,128)(2,1)} %select_select_fusion), calls=%async_computation | async-start | bytes 17694720 | tf_op jit(solution)/shard_map/all_to_all | solution.py:100
  97.3 244.0 %all-reduce.2.cloned.1.call-start = ((), (), s32[]{:S(2)}) async-start(), calls=%async_computation.5 | async-start | bytes 327680 | tf_op jit(solution)/shard_map/psum | solution.py:110
  246.9 1.6 copy-start.3
  247.8 95.0 %copy-start.1 = (bf16[240,2560]{1,0:T(8,128)(2,1)S(1)}, bf16[240,2560]{1,0:T(8,128)(2,1)}, u32[]{:S(2)}) copy-start(bf16[240,2560]{1,0:T(8,128)(2,1)} %param.8) | copy-start | bytes 3686404
Sparse Core Ops, SparseCore 0:
  9.6 224.9 all-gather.1
  249.4 91.8 all-reduce.1
where the time goes:
time: 350 us
  waiting for transfers between devices  239 us (68%)
  local copies, waits for them, and re-layouts  42 us (12%)
  matrix products  22.5 us (6%)
  starting transfers between devices  17 us (5%)
  other arithmetic  14.4 us (4%)
  between operations  14.3 us (4%)
    psum x1, waiting for transfers between devices, per_device(): grad_sum = lax.psum(grad_terms, ('dp', 'shard'))  92 us
    all_to_all x1, waiting for transfers between devices, per_device(): lax.all_to_all(rows_send, 'dp', split_axis=0, concat_axis=0, tiled=True)  91.3 us
    all_gather x1, waiting for transfers between devices, project(): lax.all_gather(out_weight, 'shard', axis=1, tiled=True)  28.8 us
    all_to_all x1, waiting for transfers between devices, per_device(): lax.all_to_all(resid_send, 'dp', split_axis=0, concat_axis=0, tiled=True)  26.7 us
    gather x1, local copies, waits for them, and re-layouts, per_device(): jnp.take(projected, row_index, axis=0)  22.4 us
    dot_general x1, matrix products, project(): jnp.dot(attended, lax.all_gather(out_weight, 'shard', axis=1, tiled=True)...  12.4 us
    select_n x1, other arithmetic, per_device(): jnp.where(live_rows[:, :, None], jnp.take(projected, row_index, axis=0), 0)  8.14 us
  transfers between devices with their start and end apart: 6, of which 4 were waited for; matrix products, arithmetic and copies ran while one was open for 18% of the time, Pallas kernels for 0%

commit v1 on v0

--- a/solution.py
+++ b/solution.py
@@ -107,7 +107,7 @@
     mixed_rows = project(attended, out_weight) + represent.astype(jnp.float32)
     hidden = (mixed_rows * keep_mask[:, None]).astype(jnp.bfloat16)
     grad_terms = probe_terms(represent, hidden, got_labels.reshape(-1), keep_mask, probe_weight)
-    grad_sum = lax.psum(grad_terms, ("dp", "shard"))
+    grad_sum = jnp.sum(lax.all_gather(grad_terms, ("dp", "shard")), axis=0)
     return (hidden, grad_sum)
 
 

time: 350 us -> 305 us (0.87)
  waiting for transfers between devices: 239 us -> 192 us
    psum x1 -> x0, waiting for transfers between devices: 92 us -> none  [per_device(): grad_sum = lax.psum(grad_terms, ('dp', 'shard'))]
    all_gather x0 -> x1, waiting for transfers between devices: none -> 44.1 us  [per_device(): grad_sum = jnp.sum(lax.all_gather(grad_terms, ('dp', 'shard')), axis=0)]
  transfers between devices with their start and end apart: 6 -> 6, of which waited for: 4 -> 4; matrix products, arithmetic and copies ran while one was open for 18% -> 21% of each run, Pallas kernels for 0% -> 0%
where the time goes in v1:
time: 305 us; the launch traced here: 303 us
  waiting for transfers between devices  192 us (63%)
  local copies, waits for them, and re-layouts  40.4 us (13%)
  matrix products  22.5 us (7%)
  starting transfers between devices  17 us (6%)
  other arithmetic  17 us (6%)
  between operations  14.3 us (5%)
    all_to_all x1, waiting for transfers between devices, per_device(): lax.all_to_all(rows_send, 'dp', split_axis=0, concat_axis=0, tiled=True)  91.3 us
    all_gather x1, waiting for transfers between devices, per_device(): grad_sum = jnp.sum(lax.all_gather(grad_terms, ('dp', 'shard')), axis=0)  44.1 us
    all_gather x1, waiting for transfers between devices, project(): lax.all_gather(out_weight, 'shard', axis=1, tiled=True)  28.8 us
    all_to_all x1, waiting for transfers between devices, per_device(): lax.all_to_all(resid_send, 'dp', split_axis=0, concat_axis=0, tiled=True)  26.7 us
    gather x1, local copies, waits for them, and re-layouts, per_device(): jnp.take(projected, row_index, axis=0)  22.4 us
    dot_general x1, matrix products, project(): jnp.dot(attended, lax.all_gather(out_weight, 'shard', axis=1, tiled=True)...  12.4 us
    select_n x1, other arithmetic, per_device(): jnp.where(live_rows[:, :, None], jnp.take(projected, row_index, axis=0), 0)  8.14 us
  transfers between devices with their start and end apart: 6, of which 4 were waited for; matrix products, arithmetic and copies ran while one was open for 21% of the time, Pallas kernels for 0%

profile of v1, /device:TPU:8, one launch (start us, length us, event | category | flops | bytes accessed | tf_op | source)
XLA Modules:
  0.0 302.7 jit_solution(11174682310982965623)
XLA Ops:
  7.2 0.7 all-gather.4.cloned.1.call-update
  8.3 0.2 fusion.37
  8.5 0.7 copy.27
  9.2 3.2 %all-to-all-start.1 = ((s32[4,1,3]{2,1,0:T(1,128)}), s32[4,1,3]{2,1,0:T(1,128)S(1)}, u32[]{:S(2)}, u32[]{:S(2)}) async-start(s32[4,1,3]{2,1,0:T(1,128)} %copy.27), calls=%async_computation.1 | async-start | bytes 4096 | tf_op jit(solution)/shard_map/all_to_all | solution.py:97
  13.4 4.2 %gather_fusion.1 = bf16[576,2560]{1,0:T(8,128)(2,1)} fusion(bf16[240,2560]{1,0:T(8,128)(2,1)S(1)} %copy-done, s32[1024]{0:T(1024)S(1)} %pad_clamp_fusion), kind=kCustom, calls=%fused_computation.1 | custom fusion | bytes 5900544 | tf_op jit(solution)/shard_map/jit(_take)/gather | solution.py:93
  17.6 3.9 %gather_fusion.2 = s32[576]{0:T(1024)S(1)} fusion(s32[240]{0:T(256)S(1)} %copy-done.2, s32[1024]{0:T(1024)S(1)} %pad_clamp_fusion), kind=kCustom, calls=%fused_computation.2 | custom fusion | bytes 6912 | tf_op jit(solution)/shard_map/jit(_take)/gather | solution.py:94
  21.6 0.6 copy.31
  22.3 3.3 %all-to-all-start.3 = ((s32[4,1,144]{2,1,0:T(1,128)}), s32[4,1,144]{2,1,0:T(1,128)S(1)}, u32[]{:S(2)}, u32[]{:S(2)}) async-start(s32[4,1,144]{2,1,0:T(1,128)} %copy.31), calls=%async_computation.3 | async-start | bytes 8192 | tf_op jit(solution)/shard_map/all_to_all | solution.py:96
  25.5 4.2 %select_select_fusion.1 = bf16[4,144,2560]{2,1,0:T(8,128)(2,1)} fusion(bf16[4,144,2560]{2,1,0:T(8,128)(2,1)} %bitcast.62, pred[4,144]{1,0:T(4,128)(4,1)S(1)} %get-tuple-element.8, pred[4,144]{1,0:T(4,128)(4,1)S(1)} %get-tuple-element.7), kind=kLoop, calls=%fused_computation.23 | loop fusion | flops 2949120 | bytes 5899392 | tf_op jit(solution)/shard_map/jit(_where)/select_n | solution.py:93
  29.7 22.4 %gather_fusion = bf16[576,7680]{1,0:T(8,128)(2,1)} fusion(bf16[240,7680]{1,0:T(8,128)(2,1)} %param.7, s32[1024]{0:T(1024)S(1)} %pad_clamp_fusion), kind=kCustom, calls=%fused_computation | custom fusion | bytes 17697024 | tf_op jit(solution)/shard_map/jit(_take)/gather | solution.py:92
  52.1 4.6 %all-to-all-start.2 = ((bf16[4,144,2560]{2,1,0:T(8,128)(2,1)}), bf16[4,144,2560]{2,1,0:T(8,128)(2,1)}, u32[]{:S(2)}, u32[]{:S(2)}) async-start(bf16[4,144,2560]{2,1,0:T(8,128)(2,1)} %select_select_fusion.1), calls=%async_computation.2 | async-start | bytes 5898240 | tf_op jit(solution)/shard_map/all_to_all | solution.py:101
  56.8 8.1 %select_select_fusion = bf16[4,144,7680]{2,1,0:T(8,128)(2,1)} fusion(bf16[4,144,7680]{2,1,0:T(8,128)(2,1)} %bitcast.61, pred[4,144]{1,0:T(4,128)(4,1)S(1)} %get-tuple-element.8, pred[4,144]{1,0:T(4,128)(4,1)S(1)} %get-tuple-element.7), kind=kLoop, calls=%fused_computation.3 | loop fusion | flops 8847360 | bytes 17695872 | tf_op jit(solution)/shard_map/jit(_where)/select_n | solution.py:92
  64.9 26.7 %all-to-all-done.2 = bf16[4,144,2560]{2,1,0:T(8,128)(2,1)} async-done(((bf16[4,144,2560]{2,1,0:T(8,128)(2,1)}), bf16[4,144,2560]{2,1,0:T(8,128)(2,1)}, u32[]{:S(2)}, u32[]{:S(2)}) %all-to-all-start.2) | async-done | bytes 2949152 | tf_op jit(solution)/shard_map/all_to_all | solution.py:101
  91.6 5.7 %all-to-all-start = ((bf16[4,144,7680]{2,1,0:T(8,128)(2,1)}), bf16[4,144,7680]{2,1,0:T(8,128)(2,1)}, u32[]{:S(2)}, u32[]{:S(2)}) async-start(bf16[4,144,7680]{2,1,0:T(8,128)(2,1)} %select_select_fusion), calls=%async_computation | async-start | bytes 17694720 | tf_op jit(solution)/shard_map/all_to_all | solution.py:100
  97.3 0.2 all-gather.6.cloned.1.call-start
  97.6 0.5 broadcast.237
  98.1 0.7 reduce.4
  99.1 2.7 fusion.43
  101.8 2.3 convolution_bitcast_fusion.1
  104.1 91.3 %all-to-all-done = bf16[4,144,7680]{2,1,0:T(8,128)(2,1)} async-done(((bf16[4,144,7680]{2,1,0:T(8,128)(2,1)}), bf16[4,144,7680]{2,1,0:T(8,128)(2,1)}, u32[]{:S(2)}, u32[]{:S(2)}) %all-to-all-start) | async-done | bytes 8847392 | tf_op jit(solution)/shard_map/all_to_all | solution.py:100
  195.4 4.0 %slice_bitcast_fusion.2 = (bf16[12,6,20,8,128]{4,3,2,1,0:T(8,128)(2,1)S(1)}, bf16[12,6,20,8,128]{4,3,2,1,0:T(8,128)(2,1)S(1)}, bf16[12,6,20,8,128]{4,3,2,1,0:T(8,128)(2,1)S(1)}) fusion(bf16[12,48,7680]{2,1,0:T(8,128)(2,1)} %bitcast.5), kind=kLoop, calls=%fused_computation.22 | loop fusion | bytes 17694720
  199.4 1.7 fusion
  201.2 2.0 convert_bitcast_fusion
  203.2 2.6 copy.30
  205.8 28.8 %all-gather.4.cloned.1.call-done = bf16[2560,2560]{1,0:T(8,128)(2,1)} async-done(((bf16[2560,640]{1,0:T(8,128)(2,1)}), bf16[2560,2560]{1,0:T(8,128)(2,1)}) %all-gather.4.cloned.1.call-update) | async-done | bytes 13107216 | tf_op jit(solution)/shard_map/all_gather | solution.py:43
  234.6 12.4 %multiply_convert_fusion = bf16[576,2560]{1,0:T(8,128)(2,1)S(1)} fusion(bf16[576,2560]{1,0:T(8,128)(2,1)} %bitcast.9, bf16[2560,2560]{1,0:T(8,128)(2,1)} %all-gather.4.cloned.1.call-done, bf16[72,8,20,128]{3,2,1,0:T(8,128)(2,1)} %bitcast.63, f32[576]{0:T(1024)S(1)} %reshape.360), kind=kOutput, calls=%fused_computation.4 | convolution fusion | flops 7555645440 | bytes 21956864 | tf_op jit(solution)/shard_map/dot_general | solution.py:41
  246.9 0.9 fusion.42
  247.8 0.5 convolution_bitcast_fusion
  248.3 0.2 copy-done.3
  248.5 0.7 pad_maximum_fusion
  249.2 44.1 %all-gather.6.cloned.1.call-done = f32[32,2560,8]{1,2,0:T(8,128)} async-done(((f32[2,2560,8]{1,2,0:T(8,128)}), f32[32,2560,8]{1,2,0:T(8,128)}) %all-gather.6.cloned.1.call-update) | async-done | bytes 2621456 | tf_op jit(solution)/shard_map/all_gather | solution.py:110
  293.3 2.5 reduce_sum.69
  (46 shorter events, 1.9 us)
Async XLA Ops:
  7.2 6.2 %copy-start = (bf16[240,2560]{1,0:T(8,128)(2,1)S(1)}, bf16[240,2560]{1,0:T(8,128)(2,1)}, u32[]{:S(2)}) copy-start(bf16[240,2560]{1,0:T(8,128)(2,1)} %param.8) | copy-start | bytes 3686404
  7.2 0.8 copy-start.5
  7.2 0.9 copy-start.6
  7.2 227.4 %all-gather.4.cloned.1.call-start = ((), (), s32[]{:S(2)}) async-start(), calls=%async_computation.4 | async-start | bytes 16384000 | tf_op jit(solution)/shard_map/all_gather | solution.py:43
  9.2 13.1 %all-to-all-start.1 = ((s32[4,1,3]{2,1,0:T(1,128)}), s32[4,1,3]{2,1,0:T(1,128)S(1)}, u32[]{:S(2)}, u32[]{:S(2)}) async-start(s32[4,1,3]{2,1,0:T(1,128)} %copy.27), calls=%async_computation.1 | async-start | bytes 4096 | tf_op jit(solution)/shard_map/all_to_all | solution.py:97
  13.4 4.2 %copy-start.2 = (s32[240]{0:T(256)S(1)}, s32[240]{0:T(256)}, u32[]{:S(2)}) copy-start(s32[240]{0:T(256)} %param.11) | copy-start | bytes 2884
  22.3 29.9 %all-to-all-start.3 = ((s32[4,1,144]{2,1,0:T(1,128)}), s32[4,1,144]{2,1,0:T(1,128)S(1)}, u32[]{:S(2)}, u32[]{:S(2)}) async-start(s32[4,1,144]{2,1,0:T(1,128)} %copy.31), calls=%async_computation.3 | async-start | bytes 8192 | tf_op jit(solution)/shard_map/all_to_all | solution.py:96
  52.1 39.5 %all-to-all-start.2 = ((bf16[4,144,2560]{2,1,0:T(8,128)(2,1)}), bf16[4,144,2560]{2,1,0:T(8,128)(2,1)}, u32[]{:S(2)}, u32[]{:S(2)}) async-start(bf16[4,144,2560]{2,1,0:T(8,128)(2,1)} %select_select_fusion.1), calls=%async_computation.2 | async-start | bytes 5898240 | tf_op jit(solution)/shard_map/all_to_all | solution.py:101
  64.9 34.2 %copy-start.4 = (bf16[2,2560,8]{1,2,0:T(8,128)(2,1)S(1)}, bf16[2,2560,8]{1,2,0:T(8,128)(2,1)}, u32[]{:S(2)}) copy-start(bf16[2,2560,8]{1,2,0:T(8,128)(2,1)} %param.10) | copy-start | bytes 245764
  91.6 103.8 %all-to-all-start = ((bf16[4,144,7680]{2,1,0:T(8,128)(2,1)}), bf16[4,144,7680]{2,1,0:T(8,128)(2,1)}, u32[]{:S(2)}, u32[]{:S(2)}) async-start(bf16[4,144,7680]{2,1,0:T(8,128)(2,1)} %select_select_fusion), calls=%async_computation | async-start | bytes 17694720 | tf_op jit(solution)/shard_map/all_to_all | solution.py:100
  97.3 196.0 %all-gather.6.cloned.1.call-start = ((), (), s32[]{:S(2)}) async-start(), calls=%async_computation.5 | async-start | bytes 2785280 | tf_op jit(solution)/shard_map/all_gather | solution.py:110
  246.9 1.6 copy-start.3
  247.8 48.0 %copy-start.1 = (bf16[240,2560]{1,0:T(8,128)(2,1)S(1)}, bf16[240,2560]{1,0:T(8,128)(2,1)}, u32[]{:S(2)}) copy-start(bf16[240,2560]{1,0:T(8,128)(2,1)} %param.8) | copy-start | bytes 3686404
Sparse Core Ops, SparseCore 0:
  9.6 224.9 all-gather.3
  249.4 43.9 all-gather.5
